TPU v7x, 32 devices: a whole 2x2x4 slice. The times are simulated.
32 devices in a mesh: sub: 4 (over y, x), row: 8 (over z, core).
Axes of the slice: x: 2, y: 2, z: 4, core: 2. Of those that a mesh axis runs over, the one named last changes fastest.
Arguments:
- inverse: float32 [4, 1024, 12288], P('sub', 'row')
- sources: float32 [4, 16, 12288], P('sub', None, 'row'), may hold values from -6 to 6
- line_history: float32 [4, 32, 1024], P('sub', None, 'row'), may hold values from -6 to 6
- line_dest: int32 [4, 1024], P('sub', 'row'), may hold values from 0 to 3, as said below
- line_port: int32 [4, 1024], P('sub', 'row'), may hold values from 0 to 1023
- line_delay: int32 [4, 1024], P('sub', 'row'), may hold values from 16 to 32
- prev_voltage: float32 [4, 1024], P('sub', 'row'), may hold values from -6 to 6
- flux_start: float32 [4, 1024], P('sub', 'row'), may hold values from -3 to 3
- arrester_gain: float32 [4, 1024], P('sub', 'row'), may hold values from 0.5 to 4
- core_gain: float32 [4, 1024], P('sub', 'row'), may hold values from 0.25 to 2
- arrester_slots: int32 [4, 128], P('sub', 'row'), may hold values from 0 to 127, as said below
- core_slots: int32 [4, 128], P('sub', 'row'), may hold values from 0 to 127, as said below
Outputs:
- voltages: float32 [4, 16, 1024], P('sub', None, 'row')
- final_flux: float32 [4, 1024], P('sub', 'row')
Inputs may be any that keep to these rules, and one draw needn't show every extreme that they name: `line_dest`: a record never names its own subnetwork; among the 128 records of one device no subnetwork is named more than 86 times, and in every such block some subnetwork is named exactly 86 times. `arrester_slots`: the 16 entries of one device are distinct slots of that device's 128 ports and share no slot with that device's core entries. `core_slots`: the 16 entries of one device are distinct slots of that device's 128 ports.
All inputs are finite; a program needn't handle non-finite values.
Results may differ from a plain program's by a relative error of at most 0.0003.
Values sent between devices are 32-bit elements; how exact they have to be, the bound alone decides.
A program may use at most 64 MiB of HBM per device.

v0:
```python
import jax
import jax.numpy as jnp
from jax import lax
from jax.sharding import PartitionSpec as P

STEPS = 16
HISTORY = 32
NEWTON = 2
half_step = 0.25
knee_volts = 1.5
cubic_term = 0.25


def element_terms(iterate, voltage, flux_now, arrester_mask, arrester_gain, core_mask, core_gain):
    linked = flux_now + half_step * (iterate + voltage)
    ratio = iterate / knee_volts
    current = arrester_mask * arrester_gain * iterate * (
        1.0 + ratio * ratio
    ) + core_mask * core_gain * (linked + cubic_term * linked * linked * linked)
    slope_now = arrester_mask * arrester_gain * (
        1.0 + 3.0 * ratio * ratio
    ) + core_mask * core_gain * half_step * (1.0 + 3.0 * cubic_term * linked * linked)
    return (current, slope_now)


def on_device(
    inverse,
    sources,
    line_history,
    line_dest,
    line_port,
    line_delay,
    prev_voltage,
    flux_start,
    arrester_gain,
    core_gain,
    arrester_slots,
    core_slots,
):
    matrix = inverse[0]
    port_rows = matrix.shape[0]
    row_count = lax.axis_size("row")
    slice_len = sources.shape[2]
    subnets = lax.axis_size("sub")
    lines_here = line_dest.shape[1]
    capacity = 2 * ((lines_here + subnets - 2) // (subnets - 1))
    target = line_dest[0]
    onehot_dest = (target[:, None] == jnp.arange(subnets, dtype=jnp.int32)[None, :]).astype(
        jnp.int32
    )
    running_rank = jnp.cumsum(onehot_dest, axis=0)
    within = jnp.sum(onehot_dest * running_rank, axis=1) - 1
    position = target * capacity + within
    placing = position[:, None] == jnp.arange(subnets * capacity, dtype=jnp.int32)[None, :]
    place_float = placing.astype(jnp.float32).reshape(lines_here, subnets, capacity)
    place_int = placing.astype(jnp.int32).reshape(lines_here, subnets, capacity)
    outgoing = jnp.einsum(
        "hl,lsc->shc", line_history[0], place_float, precision=lax.Precision.HIGHEST
    )
    port_slot = jnp.sum(place_int * (line_port[0] + 1)[:, None, None], axis=0) - 1
    delay_slot = jnp.sum(place_int * line_delay[0][:, None, None], axis=0)
    tag_block = jnp.stack([port_slot, delay_slot], axis=1)
    arrived, arrived_tags = (
        lax.all_to_all(outgoing, "sub", split_axis=0, concat_axis=0, tiled=True),
        lax.all_to_all(tag_block, "sub", split_axis=0, concat_axis=0, tiled=True),
    )
    records = subnets * capacity
    arrived_hist = jnp.transpose(arrived, (1, 0, 2)).reshape(HISTORY, records)
    arrived_port = arrived_tags[:, 0, :].reshape(records)
    arrived_delay = arrived_tags[:, 1, :].reshape(records)
    lag_index = HISTORY + jnp.arange(STEPS, dtype=jnp.int32)[:, None] - arrived_delay[None, :]
    lag_hit = jnp.arange(HISTORY, dtype=jnp.int32)[:, None, None] == lag_index[None, :, :]
    picked = jnp.sum(jnp.where(lag_hit, arrived_hist[:, None, :], 0.0), axis=0)
    landing = (
        arrived_port[:, None] == jnp.arange(row_count * port_rows, dtype=jnp.int32)[None, :]
    ).astype(jnp.float32)
    partial_value = -jnp.dot(picked, landing, precision=lax.Precision.HIGHEST)
    history = lax.psum_scatter(partial_value, "row", scatter_dimension=1, tiled=True)
    row_index = lax.axis_index("row")
    own_block = lax.dynamic_slice_in_dim(matrix, row_index * slice_len, port_rows, 1)
    self_imp = jnp.diagonal(own_block)
    arrest_here = arrester_gain[0]
    core_here = core_gain[0]
    source_rows = sources[0]
    window = jnp.concatenate(
        [source_rows[:, :port_rows] + history, source_rows[:, port_rows:]], axis=1
    )
    first_terms = lax.dot_general(
        lax.all_gather(window, "row", axis=1, tiled=True),
        matrix,
        (((1,), (1,)), ((), ())),
        precision=lax.Precision.HIGHEST,
    )
    coupling = matrix.reshape(port_rows, row_count, slice_len)[:, :, :port_rows].reshape(
        port_rows, row_count * port_rows
    )
    elem_slots = jnp.concatenate([arrester_slots[0], core_slots[0]])
    elem_count = elem_slots.shape[0]
    all_slots = lax.all_gather(elem_slots, "row", axis=0, tiled=True)
    global_ports = (
        jnp.arange(all_slots.shape[0], dtype=jnp.int32) // elem_count * port_rows + all_slots
    )
    cross_cols = jnp.take(coupling, global_ports, axis=1)
    own_rows = jnp.take(cross_cols, elem_slots, axis=0)
    arrest_flag = (jnp.arange(elem_count, dtype=jnp.int32) < arrester_slots.shape[1]).astype(
        jnp.float32
    )
    local_params = jnp.stack(
        [
            arrest_here[elem_slots],
            core_here[elem_slots],
            prev_voltage[0][elem_slots],
            flux_start[0][elem_slots],
            self_imp[elem_slots],
            arrest_flag,
        ],
        axis=1,
    )
    local_first = jnp.transpose(jnp.take(first_terms, elem_slots, axis=1))
    elem_matrix, elem_first, elem_params = (
        lax.all_gather(own_rows, "row", axis=0, tiled=True),
        lax.all_gather(local_first, "row", axis=0, tiled=True),
        lax.all_gather(local_params, "row", axis=0, tiled=True),
    )
    arrest_elem = elem_params[:, 0]
    core_elem = elem_params[:, 1]
    elem_self = elem_params[:, 4]
    elem_arrest = elem_params[:, 5]
    elem_core = 1.0 - elem_arrest

    def elem_advance(carried, first_now):
        voltage, flux_now = carried
        iterate = voltage
        current = jnp.zeros_like(voltage)
        for newton_pass in range(NEWTON):
            current, slope_now = element_terms(
                iterate, voltage, flux_now, elem_arrest, arrest_elem, elem_core, core_elem
            )
            network = first_now - jnp.dot(elem_matrix, current, precision=lax.Precision.HIGHEST)
            iterate = iterate - (iterate - network) / (1.0 + elem_self * slope_now)
        return ((iterate, flux_now + half_step * (iterate + voltage)), (iterate, current))

    (elem_last, elem_flux), (elem_volts, last_current) = lax.scan(
        elem_advance, (elem_params[:, 2], elem_params[:, 3]), jnp.transpose(elem_first)
    )
    own_volts = first_terms - lax.dot_general(
        last_current, cross_cols, (((1,), (1,)), ((), ())), precision=lax.Precision.HIGHEST
    )
    own_elem = lax.dynamic_slice_in_dim(elem_volts, row_index * elem_count, elem_count, 1)
    elem_place = (elem_slots[:, None] == jnp.arange(port_rows, dtype=jnp.int32)[None, :]).astype(
        jnp.float32
    )
    elem_here = jnp.sum(elem_place, axis=0)
    stacked = own_volts * (1.0 - elem_here) + jnp.dot(
        own_elem, elem_place, precision=lax.Precision.HIGHEST
    )
    previous = jnp.concatenate([prev_voltage[0][None, :], stacked[:-1]], axis=0)
    final_flux = flux_start[0] + half_step * jnp.sum(stacked + previous, axis=0)
    return (stacked[None], final_flux[None])


def solution(mesh):
    in_specs = (
        P("sub", "row", None),
        P("sub", None, "row"),
        P("sub", None, "row"),
        P("sub", "row"),
        P("sub", "row"),
        P("sub", "row"),
        P("sub", "row"),
        P("sub", "row"),
        P("sub", "row"),
        P("sub", "row"),
        P("sub", "row"),
        P("sub", "row"),
    )
    out_specs = (P("sub", None, "row"), P("sub", "row"))
    return jax.shard_map(
        on_device, mesh=mesh, in_specs=in_specs, out_specs=out_specs, check_vma=False
    )
```

profile of v0, /device:TPU:0, one launch (start us, length us, event | category | flops | bytes accessed | tf_op | source)
XLA Modules:
  0.0 157.2 jit_solution(13829604152136079206)
XLA Ops:
  7.2 0.7 fusion.25
  8.1 0.8 select_reduce_fusion.1
  8.9 0.7 add_add_fusion
  9.6 0.7 add_bitcast_fusion
  10.3 1.0 fusion.19
  11.2 0.6 pad_add_fusion
  11.8 5.2 %all-to-all-start = ((s32[4,2,86]{2,1,0:T(2,128)}), s32[4,2,86]{2,1,0:T(2,128)S(1)}, u32[]{:S(2)}, u32[]{:S(2)}) async-start(s32[4,2,86]{2,1,0:T(2,128)} %pad_add_fusion), calls=%async_computation | async-start | bytes 8192 | tf_op jit(solution)/shard_map/all_to_all | solution.py:65
  17.1 1.2 dynamic-slice.1
  19.0 0.8 fusion.36
  20.0 6.6 %copy.44 = f32[1,128,12288]{1,2,0:T(8,128)} copy(f32[1,128,12288]{2,1,0:T(8,128)} %param.14) | data formatting | bytes 12582912 | tf_op jit(solution)/shard_map/reshape;squeeze | solution.py:94
  26.6 0.9 dynamic-slice_bitcast_fusion
  27.6 1.2 gather_fusion.4
  28.8 0.7 gather_fusion.5
  29.5 0.7 gather_fusion
  30.2 0.7 gather_fusion.1
  30.9 0.7 gather_fusion.2
  31.6 0.7 gather_fusion.3
  32.4 14.3 %all-gather = f32[8,32,6]{1,2,0:T(8,128)S(1)} all-gather(f32[1,32,6]{1,2,0:T(8,128)S(1)} %bitcast.120), channel_id=1, replica_groups=mesh['sub'=4,'row'=8] {'row'}, dimensions={0}, use_global_device_ids=true | all-gather | bytes 6912 | tf_op jit(solution)/shard_map/all_gather | solution.py:123
  46.8 1.0 convolution_bitcast_fusion
  47.8 8.9 %all-reduce = s32[256]{0:T(256)S(1)} all-reduce(s32[256]{0:T(256)S(1)} %get-tuple-element.216), channel_id=1, replica_groups=mesh['sub'=4,'row'=8] {'row'}, use_global_device_ids=true, to_apply=%add | all-reduce | flops 256 | bytes 2048
  56.7 1.1 slice.75
  57.8 0.7 gather_fusion.7
  59.4 4.2 %all-to-all-start.1 = ((f32[4,32,86]{2,1,0:T(8,128)}), f32[4,32,86]{2,1,0:T(8,128)S(1)}, u32[]{:S(2)}, u32[]{:S(2)}) async-start(f32[4,32,86]{2,1,0:T(8,128)} %convolution_bitcast_fusion), calls=%async_computation.1 | async-start | bytes 131072 | tf_op jit(solution)/shard_map/all_to_all | solution.py:64
  63.9 4.6 %all-to-all-done.1 = f32[4,32,86]{2,1,0:T(8,128)S(1)} async-done(((f32[4,32,86]{2,1,0:T(8,128)}), f32[4,32,86]{2,1,0:T(8,128)S(1)}, u32[]{:S(2)}, u32[]{:S(2)}) %all-to-all-start.1) | async-done | bytes 44064 | tf_op jit(solution)/shard_map/all_to_all | solution.py:64
  68.7 1.2 fusion.15
  70.1 14.2 %all_gather.19 = f32[256,256]{1,0:T(8,128)S(1)} all-gather(f32[32,256]{1,0:T(8,128)S(1)} %broadcast_select_fusion), channel_id=1, replica_groups=mesh['sub'=4,'row'=8] {'row'}, dimensions={0}, use_global_device_ids=true | all-gather | bytes 294912 | tf_op jit(solution)/shard_map/all_gather | solution.py:121
  84.3 13.2 %reduce-scatter.2.cloned.1.call-done = f32[16,128]{1,0:T(8,128)} async-done(((f32[16,1024]{1,0:T(8,128)}), f32[16,128]{1,0:T(8,128)}) %reduce-scatter.2.cloned.1.call-update) | async-done | bytes 8208 | tf_op jit(solution)/shard_map/reduce_scatter | solution.py:78
  97.5 0.7 slice_add_fusion
  98.2 15.7 %all_gather.15 = f32[16,12288]{1,0:T(8,128)S(1)} all-gather(f32[16,1536]{1,0:T(8,128)S(1)} %pad_maximum_fusion), channel_id=1, replica_groups=mesh['sub'=4,'row'=8] {'row'}, dimensions={1}, use_global_device_ids=true | all-gather | bytes 884736 | tf_op jit(solution)/shard_map/all_gather | solution.py:89
  113.9 7.0 %fusion.12 = f32[16,128]{1,0:T(8,128)S(1)} fusion(f32[16,12288]{1,0:T(8,128)S(1)} %all_gather.15, f32[1,128,12288]{2,1,0:T(8,128)} %param.14), kind=kOutput, calls=%fused_computation.31 | convolution fusion | flops 301989888 | bytes 7086080 | tf_op jit(solution)/shard_map/dot_general | solution.py:88
  121.7 14.0 %all-gather.1 = f32[8,32,16]{1,2,0:T(8,128)S(1)} all-gather(f32[1,32,16]{1,2,0:T(8,128)S(1)} %copy.40), channel_id=1, replica_groups=mesh['sub'=4,'row'=8] {'row'}, dimensions={0}, use_global_device_ids=true | all-gather | bytes 18432 | tf_op jit(solution)/shard_map/all_gather | solution.py:122
  135.8 13.4 %while.19 = (s32[]{:T(128)}, f32[256]{0:T(256)S(1)}, f32[256]{0:T(256)S(1)}, f32[16,256]{1,0:T(8,128)S(1)}, f32[16,256]{1,0:T(8,128)S(1)}, /*index=5*/f32[16,256...) while((s32[]{:T(128)}, f32[256]{0:T(256)S(1)}, ...), condition=%wide.region_7.8_spmd, body=%wide.region_6.7_spmd.sunk | while | flops 1591042 | bytes 559233 | solution.py:143
  (192 shorter events, 16.8 us)
Async XLA Ops:
  7.2 39.6 %copy-start = (f32[1,32,128]{2,1,0:T(8,128)S(1)}, f32[1,32,128]{2,1,0:T(8,128)}, u32[]{:S(2)}) copy-start(f32[1,32,128]{2,1,0:T(8,128)} %param.16) | copy-start | bytes 49156
  11.8 47.6 %all-to-all-start = ((s32[4,2,86]{2,1,0:T(2,128)}), s32[4,2,86]{2,1,0:T(2,128)S(1)}, u32[]{:S(2)}, u32[]{:S(2)}) async-start(s32[4,2,86]{2,1,0:T(2,128)} %pad_add_fusion), calls=%async_computation | async-start | bytes 8192 | tf_op jit(solution)/shard_map/all_to_all | solution.py:65
  19.9 7.6 %copy-start.7 = (s32[1,16]{1,0:T(1,128)S(1)}, s32[1,16]{1,0:T(1,128)}, u32[]{:S(2)}) copy-start(s32[1,16]{1,0:T(1,128)} %param.25) | copy-start | bytes 196
  19.9 7.6 %copy-start.8 = (s32[1,16]{1,0:T(1,128)S(1)}, s32[1,16]{1,0:T(1,128)}, u32[]{:S(2)}) copy-start(s32[1,16]{1,0:T(1,128)} %param.24) | copy-start | bytes 196
  19.9 9.6 %copy-start.2 = (f32[1,128]{1,0:T(1,128)S(1)}, f32[1,128]{1,0:T(1,128)}, u32[]{:S(2)}) copy-start(f32[1,128]{1,0:T(1,128)} %param.22) | copy-start | bytes 1540
  19.9 10.3 %copy-start.3 = (f32[1,128]{1,0:T(1,128)S(1)}, f32[1,128]{1,0:T(1,128)}, u32[]{:S(2)}) copy-start(f32[1,128]{1,0:T(1,128)} %param.23) | copy-start | bytes 1540
  19.9 11.0 %copy-start.1 = (f32[1,128]{1,0:T(1,128)S(1)}, f32[1,128]{1,0:T(1,128)}, u32[]{:S(2)}) copy-start(f32[1,128]{1,0:T(1,128)} %param.20) | copy-start | bytes 1540
  20.0 11.7 %copy-start.4 = (f32[1,128]{1,0:T(1,128)S(1)}, f32[1,128]{1,0:T(1,128)}, u32[]{:S(2)}) copy-start(f32[1,128]{1,0:T(1,128)} %param.21) | copy-start | bytes 1540
  26.6 43.5 %copy-start.5 = (f32[1,16,1536]{2,1,0:T(8,128)S(1)}, f32[1,16,1536]{2,1,0:T(8,128)}, u32[]{:S(2)}) copy-start(f32[1,16,1536]{2,1,0:T(8,128)} %param.15) | copy-start | bytes 294916
  59.4 9.0 %all-to-all-start.1 = ((f32[4,32,86]{2,1,0:T(8,128)}), f32[4,32,86]{2,1,0:T(8,128)S(1)}, u32[]{:S(2)}, u32[]{:S(2)}) async-start(f32[4,32,86]{2,1,0:T(8,128)} %convolution_bitcast_fusion), calls=%async_computation.1 | async-start | bytes 131072 | tf_op jit(solution)/shard_map/all_to_all | solution.py:64
  63.6 33.8 %reduce-scatter.2.cloned.1.call-start = ((), (), s32[]{:S(2)}) async-start(), calls=%async_computation.3 | async-start | bytes 73728 | tf_op jit(solution)/shard_map/reduce_scatter | solution.py:78
  149.7 0.6 copy-start.6
Sparse Core Ops, SparseCore 0:
  70.1 27.3 reduce-scatter.1
where the time goes:
time: 158 us; the launch traced here: 157 us
  blocking collectives  67.2 us (43%)
  local copies, waits for them, and re-layouts  19.8 us (13%)
  matrix products  18.1 us (11%)
  waiting for transfers between devices  17.8 us (11%)
  between operations  14.9 us (9%)
  other arithmetic  9.39 us (6%)
  starting transfers between devices  9.39 us (6%)
    all_gather x1, blocking collectives, on_device(): lax.all_gather(window, 'row', axis=1, tiled=True)  15.7 us
    all_gather x1, blocking collectives, on_device(): lax.all_gather(local_params, 'row', axis=0, tiled=True)  14.3 us
    all_gather x1, blocking collectives, on_device(): lax.all_gather(own_rows, 'row', axis=0, tiled=True)  14.2 us
    all_gather x1, blocking collectives, on_device(): lax.all_gather(local_first, 'row', axis=0, tiled=True)  14 us
    reduce_scatter x1, waiting for transfers between devices, on_device(): lax.psum_scatter(partial_value, 'row', scatter_dimension=1, tiled=True)  13.2 us
    unnamed x1, blocking collectives  8.92 us
    dot_general x32, matrix products, elem_advance(): jnp.dot(elem_matrix, current, precision=lax.Precision.HIGHEST)  8.45 us
    dot_general x1, matrix products, on_device(): lax.dot_general(lax.all_gather(window, 'row', axis=1, tiled=True), matrix...  6.97 us
  transfers between devices with their start and end apart: 3, of which 2 were waited for; matrix products, arithmetic and copies ran while one was open for 12% of the time, Pallas kernels for 0%

commit v1 on v0

--- a/solution.py
+++ b/solution.py
@@ -2,6 +2,7 @@
 import jax.numpy as jnp
 from jax import lax
 from jax.sharding import PartitionSpec as P
+from jax.lax import all_to_all, psum
 
 STEPS = 16
 HISTORY = 32
@@ -117,8 +118,15 @@
         axis=1,
     )
     local_first = jnp.transpose(jnp.take(first_terms, elem_slots, axis=1))
+
+    def lead_heads(mesh_name, t0):
+        return jnp.concatenate(
+            all_to_all(jnp.stack([t0 for _ in range(psum(1, mesh_name))], axis=0), mesh_name, 0, 0),
+            axis=0,
+        )
+
     elem_matrix, elem_first, elem_params = (
-        lax.all_gather(own_rows, "row", axis=0, tiled=True),
+        lead_heads("row", t0=own_rows),
         lax.all_gather(local_first, "row", axis=0, tiled=True),
         lax.all_gather(local_params, "row", axis=0, tiled=True),
     )

time: 158 us -> 166 us (1.051)
  waiting for transfers between devices: 17.8 us -> 36.2 us
  blocking collectives: 67.2 us -> 52.9 us
  starting transfers between devices: 9.39 us -> 12.8 us
    reduce_scatter x1, waiting for transfers between devices: 13.2 us -> 31.6 us  [on_device(): lax.psum_scatter(partial_value, 'row', scatter_dimension=1, tiled=True)]
    all_gather x1 -> x0, blocking collectives: 14.2 us -> none  [on_device(): lax.all_gather(own_rows, 'row', axis=0, tiled=True)]
    all_to_all x0 -> x1, starting transfers between devices: none -> 3.41 us  [lead_heads(): all_to_all(jnp.stack([t0 for _ in range(psum(1, mesh_name))], axis=0), me...]
  transfers between devices with their start and end apart: 3 -> 4, of which waited for: 2 -> 2; matrix products, arithmetic and copies ran while one was open for 12% -> 17% of each run, Pallas kernels for 0% -> 0%
where the time goes in v1:
time: 166 us
  blocking collectives  52.9 us (32%)
  waiting for transfers between devices  36.2 us (22%)
  local copies, waits for them, and re-layouts  20.5 us (12%)
  matrix products  18.1 us (11%)
  between operations  14.9 us (9%)
  starting transfers between devices  12.8 us (8%)
  other arithmetic  9.39 us (6%)
    reduce_scatter x1, waiting for transfers between devices, on_device(): lax.psum_scatter(partial_value, 'row', scatter_dimension=1, tiled=True)  31.6 us
    all_gather x1, blocking collectives, on_device(): lax.all_gather(window, 'row', axis=1, tiled=True)  15.7 us
    all_gather x1, blocking collectives, on_device(): lax.all_gather(local_params, 'row', axis=0, tiled=True)  14.3 us
    all_gather x1, blocking collectives, on_device(): lax.all_gather(local_first, 'row', axis=0, tiled=True)  14 us
    unnamed x1, blocking collectives  8.92 us
    dot_general x32, matrix products, elem_advance(): jnp.dot(elem_matrix, current, precision=lax.Precision.HIGHEST)  8.45 us
    dot_general x1, matrix products, on_device(): lax.dot_general(lax.all_gather(window, 'row', axis=1, tiled=True), matrix...  6.97 us
    another operation x1, local copies, waits for them, and re-layouts, on_device(): matrix.reshape(port_rows, row_count, slice_len)[:, :, :port_rows]  6.62 us
  transfers between devices with their start and end apart: 4, of which 2 were waited for; matrix products, arithmetic and copies ran while one was open for 17% of the time, Pallas kernels for 0%

profile of v1, /device:TPU:0, one launch (start us, length us, event | category | flops | bytes accessed | tf_op | source)
XLA Modules:
  0.0 165.6 jit_solution(4196994203992272681)
XLA Ops:
  7.2 0.7 fusion.25
  8.1 0.8 select_reduce_fusion.1
  8.9 0.7 add_add_fusion
  9.6 0.7 add_bitcast_fusion
  10.3 1.0 fusion.19
  11.8 5.2 %all-to-all-start = ((s32[4,2,86]{2,1,0:T(2,128)}), s32[4,2,86]{2,1,0:T(2,128)S(1)}, u32[]{:S(2)}, u32[]{:S(2)}) async-start(s32[4,2,86]{2,1,0:T(2,128)} %pad_add_fusion), calls=%async_computation | async-start | bytes 8192 | tf_op jit(solution)/shard_map/all_to_all | solution.py:66
  17.1 1.2 dynamic-slice.1
  19.0 0.8 fusion.36
  20.0 6.6 %copy.44 = f32[1,128,12288]{1,2,0:T(8,128)} copy(f32[1,128,12288]{2,1,0:T(8,128)} %param.14) | data formatting | bytes 12582912 | tf_op jit(solution)/shard_map/reshape;squeeze | solution.py:95
  26.6 0.9 dynamic-slice_bitcast_fusion
  27.6 1.2 gather_fusion.4
  28.8 0.7 gather_fusion.5
  29.5 0.7 gather_fusion
  30.2 0.7 gather_fusion.1
  30.9 0.7 gather_fusion.2
  31.6 0.7 gather_fusion.3
  32.4 14.3 %all-gather = f32[8,32,6]{1,2,0:T(8,128)S(1)} all-gather(f32[1,32,6]{1,2,0:T(8,128)S(1)} %bitcast.122), channel_id=1, replica_groups=mesh['sub'=4,'row'=8] {'row'}, dimensions={0}, use_global_device_ids=true | all-gather | bytes 6912 | tf_op jit(solution)/shard_map/all_gather | solution.py:131
  46.8 1.0 convolution_bitcast_fusion
  47.8 8.9 %all-reduce = s32[256]{0:T(256)S(1)} all-reduce(s32[256]{0:T(256)S(1)} %get-tuple-element.216), channel_id=1, replica_groups=mesh['sub'=4,'row'=8] {'row'}, use_global_device_ids=true, to_apply=%add | all-reduce | flops 256 | bytes 2048
  56.7 1.1 slice.75
  57.8 0.7 gather_fusion.7
  59.5 4.2 %all-to-all-start.1 = ((f32[4,32,86]{2,1,0:T(8,128)}), f32[4,32,86]{2,1,0:T(8,128)S(1)}, u32[]{:S(2)}, u32[]{:S(2)}) async-start(f32[4,32,86]{2,1,0:T(8,128)} %convolution_bitcast_fusion), calls=%async_computation.1 | async-start | bytes 131072 | tf_op jit(solution)/shard_map/all_to_all | solution.py:65
  63.9 4.6 %all-to-all-done.1 = f32[4,32,86]{2,1,0:T(8,128)S(1)} async-done(((f32[4,32,86]{2,1,0:T(8,128)}), f32[4,32,86]{2,1,0:T(8,128)S(1)}, u32[]{:S(2)}, u32[]{:S(2)}) %all-to-all-start.1) | async-done | bytes 44064 | tf_op jit(solution)/shard_map/all_to_all | solution.py:65
  68.5 0.7 stack.45
  69.2 3.4 %all-to-all-start.2 = ((f32[8,32,256]{2,1,0:T(8,128)}), f32[8,32,256]{2,1,0:T(8,128)S(1)}, u32[]{:S(2)}, u32[]{:S(2)}) async-start(f32[8,32,256]{2,1,0:T(8,128)} %stack.45), calls=%async_computation.3 | async-start | bytes 524288 | tf_op jit(solution)/shard_map/all_to_all | solution.py:124
  73.0 1.2 fusion.15
  74.2 31.6 %reduce-scatter.2.cloned.1.call-done = f32[16,128]{1,0:T(8,128)} async-done(((f32[16,1024]{1,0:T(8,128)}), f32[16,128]{1,0:T(8,128)}) %reduce-scatter.2.cloned.1.call-update) | async-done | bytes 8208 | tf_op jit(solution)/shard_map/reduce_scatter | solution.py:79
  105.9 0.7 slice_add_fusion
  106.6 15.7 %all_gather.12 = f32[16,12288]{1,0:T(8,128)S(1)} all-gather(f32[16,1536]{1,0:T(8,128)S(1)} %pad_maximum_fusion), channel_id=1, replica_groups=mesh['sub'=4,'row'=8] {'row'}, dimensions={1}, use_global_device_ids=true | all-gather | bytes 884736 | tf_op jit(solution)/shard_map/all_gather | solution.py:90
  122.3 7.0 %fusion.12 = f32[16,128]{1,0:T(8,128)S(1)} fusion(f32[16,12288]{1,0:T(8,128)S(1)} %all_gather.12, f32[1,128,12288]{2,1,0:T(8,128)} %param.14), kind=kOutput, calls=%fused_computation.31 | convolution fusion | flops 301989888 | bytes 7086080 | tf_op jit(solution)/shard_map/dot_general | solution.py:89
  130.1 14.0 %all-gather.1 = f32[8,32,16]{1,2,0:T(8,128)S(1)} all-gather(f32[1,32,16]{1,2,0:T(8,128)S(1)} %copy.40), channel_id=1, replica_groups=mesh['sub'=4,'row'=8] {'row'}, dimensions={0}, use_global_device_ids=true | all-gather | bytes 18432 | tf_op jit(solution)/shard_map/all_gather | solution.py:130
  144.2 13.4 %while.19 = (s32[]{:T(128)}, f32[256]{0:T(256)S(1)}, f32[256]{0:T(256)S(1)}, f32[16,256]{1,0:T(8,128)S(1)}, f32[16,256]{1,0:T(8,128)S(1)}, /*index=5*/f32[16,256...) while((s32[]{:T(128)}, f32[256]{0:T(256)S(1)}, ...), condition=%wide.region_7.8_spmd, body=%wide.region_6.7_spmd.sunk | while | flops 1591042 | bytes 559233 | solution.py:151
  (194 shorter events, 17.4 us)
Async XLA Ops:
  7.2 39.6 %copy-start = (f32[1,32,128]{2,1,0:T(8,128)S(1)}, f32[1,32,128]{2,1,0:T(8,128)}, u32[]{:S(2)}) copy-start(f32[1,32,128]{2,1,0:T(8,128)} %param.16) | copy-start | bytes 49156
  11.8 47.6 %all-to-all-start = ((s32[4,2,86]{2,1,0:T(2,128)}), s32[4,2,86]{2,1,0:T(2,128)S(1)}, u32[]{:S(2)}, u32[]{:S(2)}) async-start(s32[4,2,86]{2,1,0:T(2,128)} %pad_add_fusion), calls=%async_computation | async-start | bytes 8192 | tf_op jit(solution)/shard_map/all_to_all | solution.py:66
  19.9 7.6 %copy-start.7 = (s32[1,16]{1,0:T(1,128)S(1)}, s32[1,16]{1,0:T(1,128)}, u32[]{:S(2)}) copy-start(s32[1,16]{1,0:T(1,128)} %param.25) | copy-start | bytes 196
  19.9 7.6 %copy-start.8 = (s32[1,16]{1,0:T(1,128)S(1)}, s32[1,16]{1,0:T(1,128)}, u32[]{:S(2)}) copy-start(s32[1,16]{1,0:T(1,128)} %param.24) | copy-start | bytes 196
  19.9 9.6 %copy-start.2 = (f32[1,128]{1,0:T(1,128)S(1)}, f32[1,128]{1,0:T(1,128)}, u32[]{:S(2)}) copy-start(f32[1,128]{1,0:T(1,128)} %param.22) | copy-start | bytes 1540
  19.9 10.3 %copy-start.3 = (f32[1,128]{1,0:T(1,128)S(1)}, f32[1,128]{1,0:T(1,128)}, u32[]{:S(2)}) copy-start(f32[1,128]{1,0:T(1,128)} %param.23) | copy-start | bytes 1540
  19.9 11.0 %copy-start.1 = (f32[1,128]{1,0:T(1,128)S(1)}, f32[1,128]{1,0:T(1,128)}, u32[]{:S(2)}) copy-start(f32[1,128]{1,0:T(1,128)} %param.20) | copy-start | bytes 1540
  20.0 11.7 %copy-start.4 = (f32[1,128]{1,0:T(1,128)S(1)}, f32[1,128]{1,0:T(1,128)}, u32[]{:S(2)}) copy-start(f32[1,128]{1,0:T(1,128)} %param.21) | copy-start | bytes 1540
  26.6 32.9 %copy-start.5 = (f32[1,16,1536]{2,1,0:T(8,128)S(1)}, f32[1,16,1536]{2,1,0:T(8,128)}, u32[]{:S(2)}) copy-start(f32[1,16,1536]{2,1,0:T(8,128)} %param.15) | copy-start | bytes 294916
  59.5 9.0 %all-to-all-start.1 = ((f32[4,32,86]{2,1,0:T(8,128)}), f32[4,32,86]{2,1,0:T(8,128)S(1)}, u32[]{:S(2)}, u32[]{:S(2)}) async-start(f32[4,32,86]{2,1,0:T(8,128)} %convolution_bitcast_fusion), calls=%async_computation.1 | async-start | bytes 131072 | tf_op jit(solution)/shard_map/all_to_all | solution.py:65
  69.2 75.0 %all-to-all-start.2 = ((f32[8,32,256]{2,1,0:T(8,128)}), f32[8,32,256]{2,1,0:T(8,128)S(1)}, u32[]{:S(2)}, u32[]{:S(2)}) async-start(f32[8,32,256]{2,1,0:T(8,128)} %stack.45), calls=%async_computation.3 | async-start | bytes 524288 | tf_op jit(solution)/shard_map/all_to_all | solution.py:124
  72.7 33.2 %reduce-scatter.2.cloned.1.call-start = ((), (), s32[]{:S(2)}) async-start(), calls=%async_computation.4 | async-start | bytes 73728 | tf_op jit(solution)/shard_map/reduce_scatter | solution.py:79
  158.1 0.6 copy-start.6
Sparse Core Ops, SparseCore 0:
  75.7 30.1 reduce-scatter.1
